TPU v7x, 256 devices: a whole 4x4x8 slice. The times are simulated.
256 devices in a mesh: tm: 4 (over y), det: 64 (over z, x, core).
Axes of the slice: x: 4, y: 4, z: 8, core: 2. Of those that a mesh axis runs over, the one named last changes fastest.
Arguments:
- offset_amplitude_array: float32 [128, 16], P('det', 'tm'), may hold values from -6 to 6
- system_remainder: float32 [128, 16], P('det', 'tm'), may hold values from -6 to 6
- conjugate_heading: float32 [128, 16], P('det', 'tm'), may hold values from -6 to 6
- region_cell_numbers: int32 [128, 16384], P('det', 'tm'), may hold values from 0 to 255
- stokes_reading_rotation: float32 [128, 16384], P('det', 'tm'), may hold values from -3.140625 to 3.140625
- scan_patch_places: int32 [128, 128], P('det', 'tm'), may hold values from 0 to 127
- holder_visited_regions: int32 [4, 64, 64, 2], P('tm', 'det'), may hold values from 0 to 47, as said below
- stokes_precision_matrices: float32 [3072, 6, 256], P('det'), as said below
Outputs:
- refreshed_offset_amplitudes: float32 [128, 16], P('det', 'tm')
- updated_residual_vector: float32 [128, 16], P('det', 'tm')
- updated_search_direction: float32 [128, 16], P('det', 'tm')
Inputs may be any that keep to these rules, and one draw needn't show every extreme that they name: For each device (i, j) and owner o, holder_visited_regions[i, j, o, :] holds 2 distinct local submaps. `stokes_precision_matrices`: each pixel's 3x3 block is symmetric positive definite.
All inputs are finite; a program needn't handle non-finite values.
Results may differ from a plain program's by a relative error of at most 0.00005.
Values sent between devices are 32-bit elements; how exact they have to be, the bound alone decides.
No kernel may reach another device: no remote copies, remote signals or barrier semaphores. Data moves between devices by JAX's collectives and lax.ppermute only.
A program may use at most 64 MiB of HBM per device.

v0:
```python
import jax
import jax.numpy as jnp
from jax import lax
from jax.sharding import PartitionSpec as P

TILE = 128
WINDOW = 256
stiffness = 0.5


def extended(value, sides, width):
    for axis, dim in sides:
        peers, length = (lax.axis_size(axis), value.shape[dim])
        up = [(i, (i + 1) % peers) for i in range(peers - 1)]
        down = [(j, i) for i, j in up]
        last = lax.slice_in_dim(value, length - width, length, axis=dim)
        leading = lax.slice_in_dim(value, 0, width, axis=dim)
        before = lax.ppermute(last, axis, up)
        after = lax.ppermute(leading, axis, down)
        value = jnp.concatenate([before, value, after], axis=dim)
    return value


def solve_blocks(binned, stokes_precision_matrices):
    first = binned[:, 0]
    second = binned[:, 1]
    third = binned[:, 2]
    out_first = (
        stokes_precision_matrices[:, 0] * first
        + stokes_precision_matrices[:, 1] * second
        + stokes_precision_matrices[:, 2] * third
    )
    out_second = (
        stokes_precision_matrices[:, 1] * first
        + stokes_precision_matrices[:, 3] * second
        + stokes_precision_matrices[:, 4] * third
    )
    out_third = (
        stokes_precision_matrices[:, 2] * first
        + stokes_precision_matrices[:, 4] * second
        + stokes_precision_matrices[:, 5] * third
    )
    return jnp.stack([out_first, out_second, out_third], axis=1)


def shards(
    offset_amplitude_array,
    system_remainder,
    conjugate_heading,
    region_cell_numbers,
    stokes_reading_rotation,
    scan_patch_places,
    holder_visited_regions,
    stokes_precision_matrices,
):
    det_dev, base_dev = conjugate_heading.shape
    samp_dev = region_cell_numbers.shape[1]
    per_owner = holder_visited_regions.shape[3]
    owners = lax.axis_size("det")
    slot_count = owners * per_owner
    sub_dev = stokes_precision_matrices.shape[0]
    cells = 3 * WINDOW
    stream = jnp.repeat(conjugate_heading, samp_dev // base_dev, axis=1)
    twice = 2.0 * stokes_reading_rotation
    cos_weight = jnp.cos(twice)
    sin_weight = jnp.sin(twice)
    slot_index = jnp.repeat(scan_patch_places, TILE, axis=1)
    cell = slot_index * cells + region_cell_numbers
    values = jnp.concatenate(
        [stream.ravel(), (stream * cos_weight).ravel(), (stream * sin_weight).ravel()]
    )
    targets = jnp.concatenate([cell.ravel(), (cell + WINDOW).ravel(), (cell + 2 * WINDOW).ravel()])
    local_bins = jax.ops.segment_sum(values, targets, num_segments=slot_count * cells).reshape(
        slot_count, cells
    )
    my_hits = holder_visited_regions.reshape(owners, per_owner)
    global_ids = jnp.arange(slot_count, dtype=jnp.int32) // per_owner * sub_dev + my_hits.reshape(
        -1
    )
    selector = (
        global_ids[None, :] == jnp.arange(sub_dev * owners, dtype=jnp.int32)[:, None]
    ).astype(jnp.float32)
    full_bins = jnp.dot(
        selector, local_bins, precision=lax.Precision.HIGHEST, preferred_element_type=jnp.float32
    )
    owned = lax.psum_scatter(full_bins, "det", scatter_dimension=0, tiled=True)
    binned = lax.psum(owned, "tm")
    sky_map = solve_blocks(binned.reshape(sub_dev, 3, WINDOW), stokes_precision_matrices).reshape(
        sub_dev, cells
    )
    whole_sky = lax.all_gather(sky_map, "det", axis=0, tiled=True)
    slot_sky = jnp.dot(
        selector.T, whole_sky, precision=lax.Precision.HIGHEST, preferred_element_type=jnp.float32
    )
    flat_sky = slot_sky.reshape(-1)
    scanned = (
        flat_sky[cell]
        + cos_weight * flat_sky[cell + WINDOW]
        + sin_weight * flat_sky[cell + 2 * WINDOW]
    )
    folded = scanned.reshape(det_dev, base_dev, samp_dev // base_dev).sum(axis=2) / (
        samp_dev // base_dev
    )
    padded = extended(conjugate_heading, (("tm", 1),), 1)
    applied = (
        conjugate_heading
        + folded
        + stiffness * (2.0 * conjugate_heading - padded[:, :-2] - padded[:, 2:])
    )
    norm_now, curvature = lax.psum(
        (jnp.sum(system_remainder * system_remainder), jnp.sum(conjugate_heading * applied)),
        ("tm", "det"),
    )
    conjugate_update_factor = norm_now / curvature
    updated_residual_vector = system_remainder - conjugate_update_factor * applied
    norm_next = lax.psum(jnp.sum(updated_residual_vector * updated_residual_vector), ("tm", "det"))
    refreshed_offset_amplitudes = (
        offset_amplitude_array + conjugate_update_factor * conjugate_heading
    )
    updated_search_direction = updated_residual_vector + norm_next / norm_now * conjugate_heading
    return (refreshed_offset_amplitudes, updated_residual_vector, updated_search_direction)


def solution(mesh):
    return jax.shard_map(
        shards,
        mesh=mesh,
        in_specs=(
            P("det", "tm"),
            P("det", "tm"),
            P("det", "tm"),
            P("det", "tm"),
            P("det", "tm"),
            P("det", "tm"),
            P("tm", "det", None, None),
            P("det", None, None),
        ),
        out_specs=(P("det", "tm"), P("det", "tm"), P("det", "tm")),
        check_vma=False,
    )
```

profile of v0, /device:TPU:1, one launch (start us, length us, event | category | flops | bytes accessed | tf_op | source)
XLA Modules:
  0.0 786.4 jit_solution(1612959436937574905)
XLA Ops:
  7.2 0.7 broadcast_multiply_fusion
  7.9 0.1 broadcast_bitcast_fusion.2
  8.0 0.8 fusion.12
  8.9 0.8 broadcast_bitcast_fusion.1
  9.7 1.2 multiply_bitcast_fusion.1
  11.0 169.6 %scatter_custom_fusion = f32[98304]{0:T(1024)S(1)} fusion(s32[24576]{0:T(1024)S(1)} %pad_add_fusion, f32[24576]{0:T(1024)S(1)} %pad_maximum_fusion.1, f32[]{:T(128)} %constant.14.clone.1), kind=kCustom, calls=%fused_computation.10 | custom fusion | flops 24576 | bytes 393220 | tf_op jit(solution)/shard_map/scatter-add | solution.py:73
  180.6 0.1 reshape.67
  180.7 0.8 copy.13
  181.4 0.1 reshape_reshape.6
  181.6 6.2 fusion.1
  187.9 155.1 %reduce-scatter.2.cloned.1.call-done = f32[48,768]{1,0:T(8,128)} async-done(((f32[3072,768]{1,0:T(8,128)}), f32[48,768]{1,0:T(8,128)}) %reduce-scatter.2.cloned.1.call-update) | async-done | bytes 147472 | tf_op jit(solution)/shard_map/reduce_scatter | solution.py:86
  343.0 1.6 reshape.68
  344.7 47.9 %all-reduce.3.cloned.1.call-done = f32[48,3,256]{2,1,0:T(4,128)} async-done(((f32[48,3,256]{2,1,0:T(4,128)}), f32[48,3,256]{2,1,0:T(4,128)}) %all-reduce.3.cloned.1.call-update) | async-done | bytes 147472 | tf_op jit(solution)/shard_map/psum | solution.py:87
  392.6 1.4 fusion.10
  394.1 0.1 pad_maximum_fusion
  394.2 0.7 copy.31
  395.0 2.2 collective-permute-start
  397.3 1.3 collective-permute-start.1
  398.6 3.0 collective-permute-done.1
  401.6 0.1 pad_maximum_fusion.2
  401.7 80.8 %all-gather.2.cloned.1.call-done = f32[3072,768]{1,0:T(8,128)} async-done(((f32[48,768]{1,0:T(8,128)}), f32[3072,768]{1,0:T(8,128)}) %all-gather.2.cloned.1.call-update) | async-done | bytes 9437200 | tf_op jit(solution)/shard_map/all_gather | solution.py:91
  482.5 7.3 fusion
  489.9 45.5 %gather_fusion = f32[8192]{0:T(1024)S(1)} fusion(f32[98304]{0:T(1024)S(1)} %reshape.70, s32[8192]{0:T(1024)S(1)} %broadcast_clamp_fusion.2), kind=kCustom, calls=%fused_computation | custom fusion | bytes 98304 | tf_op jit(solution)/shard_map/gather | solution.py:97
  535.4 45.5 %gather_fusion.1 = f32[8192]{0:T(1024)S(1)} fusion(f32[98304]{0:T(1024)S(1)} %reshape.70, s32[8192]{0:T(1024)S(1)} %broadcast_clamp_fusion.1), kind=kCustom, calls=%fused_computation.1 | custom fusion | bytes 98304 | tf_op jit(solution)/shard_map/gather | solution.py:98
  581.1 45.5 %gather_fusion.2 = f32[8192]{0:T(1024)S(1)} fusion(f32[98304]{0:T(1024)S(1)} %reshape.70, s32[8192]{0:T(1024)S(1)} %broadcast_clamp_fusion), kind=kCustom, calls=%fused_computation.2 | custom fusion | bytes 98304 | tf_op jit(solution)/shard_map/gather | solution.py:99
  626.6 0.5 multiply_add_fusion
  627.2 0.1 reduce_sum.37
  627.3 0.7 multiply_reduce_fusion.1
  627.9 74.6 %all-reduce = (f32[]{:T(128)}, f32[]{:T(128)}) all-reduce(f32[]{:T(128)} %get-tuple-element.34, f32[]{:T(128)} %get-tuple-element.7), channel_id=1, replica_groups=mesh['tm'=4,'det'=64] {'tm','det'}, use_global_device_ids=true, to_apply=%region_1.2 | all-reduce | flops 2 | bytes 16 | tf_op jit(solution)/shard_map/psum | solution.py:110
  703.9 0.6 multiply_reduce_fusion
  704.5 73.4 %psum.31 = f32[]{:T(128)} all-reduce(f32[]{:T(128)} %get-tuple-element.5), channel_id=1, replica_groups=mesh['tm'=4,'det'=64] {'tm','det'}, use_global_device_ids=true, to_apply=%region_9.10 | all-reduce | flops 1 | bytes 8 | tf_op jit(solution)/shard_map/psum | solution.py:116
  779.2 0.6 multiply_add_fusion.1
  (43 shorter events, 0.6 us)
Async XLA Ops:
  7.2 335.8 %reduce-scatter.2.cloned.1.call-start = ((), (), s32[]{:S(2)}) async-start(), calls=%async_computation.1 | async-start | bytes 9584640 | tf_op jit(solution)/shard_map/reduce_scatter | solution.py:86
  181.6 163.1 %copy-start = (f32[48,6,256]{2,0,1:T(8,128)S(1)}, f32[48,6,256]{2,0,1:T(8,128)}, u32[]{:S(2)}) copy-start(f32[48,6,256]{2,0,1:T(8,128)} %param.15) | copy-start | bytes 884740
  187.8 207.2 %copy-start.2 = (f32[2,4]{1,0:T(2,128)S(1)}, f32[2,4]{1,0:T(2,128)}, u32[]{:S(2)}) copy-start(f32[2,4]{1,0:T(2,128)} %param.10) | copy-start | bytes 100
  187.8 204.8 %all-reduce.3.cloned.1.call-start = ((), (), s32[]{:S(2)}) async-start(), calls=%async_computation.2 | async-start | bytes 393216 | tf_op jit(solution)/shard_map/psum | solution.py:87
  344.6 137.9 %all-gather.2.cloned.1.call-start = ((), (), s32[]{:S(2)}) async-start(), calls=%async_computation.3 | async-start | bytes 9584640 | tf_op jit(solution)/shard_map/all_gather | solution.py:91
  395.0 3.6 collective-permute-start
  397.3 4.4 collective-permute-start.1
  581.0 45.6 %copy-start.1 = (f32[2,4096]{1,0:T(2,128)S(1)}, f32[2,4096]{1,0:T(2,128)}, u32[]{:S(2)}) copy-start(f32[2,4096]{1,0:T(2,128)} %param.12) | copy-start | bytes 98308
  581.0 46.2 %copy-start.3 = (f32[2,4]{1,0:T(2,128)S(1)}, f32[2,4]{1,0:T(2,128)}, u32[]{:S(2)}) copy-start(f32[2,4]{1,0:T(2,128)} %param.9) | copy-start | bytes 100
  581.0 198.2 %copy-start.5 = (f32[2,4]{1,0:T(2,128)S(1)}, f32[2,4]{1,0:T(2,128)}, u32[]{:S(2)}) copy-start(f32[2,4]{1,0:T(2,128)} %param.8) | copy-start | bytes 100
  704.5 75.3 %copy-start.4 = (f32[2,4]{1,0:T(2,128)}, f32[2,4]{1,0:T(2,128)S(1)}, u32[]{:S(2)}) copy-start(f32[2,4]{1,0:T(2,128)S(1)} %get-tuple-element.6) | copy-start | bytes 100
Sparse Core Ops, SparseCore 0:
  187.9 154.9 reduce-scatter.1
  345.3 47.3 all-reduce.2
  395.4 87.0 all-gather.1
where the time goes:
time: 787 us; the launch traced here: 786 us
  waiting for transfers between devices  287 us (36%)
  other arithmetic  176 us (22%)
  blocking collectives  148 us (19%)
  local copies, waits for them, and re-layouts  141 us (18%)
  between operations  16.7 us (2%)
  matrix products  13.5 us (2%)
    scatter-add x1, other arithmetic, shards(): jax.ops.segment_sum(values, targets, num_segments=slot_count * cells)  170 us
    reduce_scatter x1, waiting for transfers between devices, shards(): owned = lax.psum_scatter(full_bins, 'det', scatter_dimension=0, tiled=True)  155 us
    all_gather x1, waiting for transfers between devices, shards(): whole_sky = lax.all_gather(sky_map, 'det', axis=0, tiled=True)  80.8 us
    psum x1, blocking collectives, shards(): lax.psum((jnp.sum(system_remainder * system_remainder), jnp.sum(conjugate...  74.6 us
    psum x1, blocking collectives, shards(): lax.psum(jnp.sum(updated_residual_vector * updated_residual_vector), ('tm...  73.4 us
    psum x1, waiting for transfers between devices, shards(): binned = lax.psum(owned, 'tm')  47.9 us
    gather x2, local copies, waits for them, and re-layouts, shards(): flat_sky[cell] + cos_weight * flat_sky[cell + WINDOW]  45.6 us
    gather x2, local copies, waits for them, and re-layouts, shards(): flat_sky[cell + WINDOW]  45.6 us
  transfers between devices with their start and end apart: 5, of which 4 were waited for; matrix products, arithmetic and copies ran while one was open for 0% of the time, Pallas kernels for 0%

commit v1 on v0

--- a/solution.py
+++ b/solution.py
@@ -6,6 +6,11 @@
 TILE = 128
 WINDOW = 256
 stiffness = 0.5
+
+
+def axis_by_axis(x, inner_axis, outer_axis):
+    inner = lax.psum(x, inner_axis)
+    return lax.psum(inner, outer_axis)
 
 
 def extended(value, sides, width):
@@ -107,9 +112,10 @@
         + folded
         + stiffness * (2.0 * conjugate_heading - padded[:, :-2] - padded[:, 2:])
     )
-    norm_now, curvature = lax.psum(
+    norm_now, curvature = axis_by_axis(
         (jnp.sum(system_remainder * system_remainder), jnp.sum(conjugate_heading * applied)),
-        ("tm", "det"),
+        "det",
+        "tm",
     )
     conjugate_update_factor = norm_now / curvature
     updated_residual_vector = system_remainder - conjugate_update_factor * applied

time: 787 us -> 848 us (1.078)
  blocking collectives: 148 us -> 209 us
    psum x1 -> x2, blocking collectives: 74.6 us -> 133 us  [the longest x1 124 us: axis_by_axis(): inner = lax.psum(x, inner_axis)]
where the time goes in v1:
time: 848 us; the launch traced here: 847 us
  waiting for transfers between devices  287 us (34%)
  blocking collectives  209 us (25%)
  other arithmetic  176 us (21%)
  local copies, waits for them, and re-layouts  141 us (17%)
  between operations  16.7 us (2%)
  matrix products  13.5 us (2%)
    scatter-add x1, other arithmetic, shards(): jax.ops.segment_sum(values, targets, num_segments=slot_count * cells)  170 us
    reduce_scatter x1, waiting for transfers between devices, shards(): owned = lax.psum_scatter(full_bins, 'det', scatter_dimension=0, tiled=True)  155 us
    psum x1, blocking collectives, axis_by_axis(): inner = lax.psum(x, inner_axis)  124 us
    all_gather x1, waiting for transfers between devices, shards(): whole_sky = lax.all_gather(sky_map, 'det', axis=0, tiled=True)  80.8 us
    psum x1, blocking collectives, shards(): lax.psum(jnp.sum(updated_residual_vector * updated_residual_vector), ('tm...  75.3 us
    psum x1, waiting for transfers between devices, shards(): binned = lax.psum(owned, 'tm')  47.9 us
    gather x2, local copies, waits for them, and re-layouts, shards(): flat_sky[cell] + cos_weight * flat_sky[cell + WINDOW]  45.6 us
    gather x2, local copies, waits for them, and re-layouts, shards(): flat_sky[cell + WINDOW]  45.6 us
  transfers between devices with their start and end apart: 5, of which 4 were waited for; matrix products, arithmetic and copies ran while one was open for 0% of the time, Pallas kernels for 0%

profile of v1, /device:TPU:1, one launch (start us, length us, event | category | flops | bytes accessed | tf_op | source)
XLA Modules:
  0.0 847.0 jit_solution(13214989791873277116)
XLA Ops:
  7.2 0.7 broadcast_multiply_fusion
  8.0 0.8 fusion.12
  8.9 0.8 broadcast_bitcast_fusion.1
  9.7 1.2 multiply_bitcast_fusion.1
  11.0 169.6 %scatter_custom_fusion = f32[98304]{0:T(1024)S(1)} fusion(s32[24576]{0:T(1024)S(1)} %pad_add_fusion, f32[24576]{0:T(1024)S(1)} %pad_maximum_fusion.1, f32[]{:T(128)} %constant.14.clone.1), kind=kCustom, calls=%fused_computation.10 | custom fusion | flops 24576 | bytes 393220 | tf_op jit(solution)/shard_map/scatter-add | solution.py:78
  180.6 0.1 reshape.67
  180.7 0.8 copy.13
  181.4 0.1 reshape_reshape.6
  181.6 6.2 fusion.1
  187.9 155.1 %reduce-scatter.2.cloned.1.call-done = f32[48,768]{1,0:T(8,128)} async-done(((f32[3072,768]{1,0:T(8,128)}), f32[48,768]{1,0:T(8,128)}) %reduce-scatter.2.cloned.1.call-update) | async-done | bytes 147472 | tf_op jit(solution)/shard_map/reduce_scatter | solution.py:91
  343.0 1.7 reshape.68
  344.7 47.9 %all-reduce.4.cloned.1.call-done = f32[48,3,256]{2,1,0:T(4,128)} async-done(((f32[48,3,256]{2,1,0:T(4,128)}), f32[48,3,256]{2,1,0:T(4,128)}) %all-reduce.4.cloned.1.call-update) | async-done | bytes 147472 | tf_op jit(solution)/shard_map/psum | solution.py:92
  392.6 1.4 fusion.10
  394.1 0.1 pad_maximum_fusion
  394.2 0.7 copy.31
  395.0 2.2 collective-permute-start
  397.2 1.3 collective-permute-start.1
  398.6 3.0 collective-permute-done.1
  401.6 0.1 pad_maximum_fusion.2
  401.7 80.8 %all-gather.2.cloned.1.call-done = f32[3072,768]{1,0:T(8,128)} async-done(((f32[48,768]{1,0:T(8,128)}), f32[3072,768]{1,0:T(8,128)}) %all-gather.2.cloned.1.call-update) | async-done | bytes 9437200 | tf_op jit(solution)/shard_map/all_gather | solution.py:96
  482.5 7.3 fusion
  489.9 45.5 %gather_fusion = f32[8192]{0:T(1024)S(1)} fusion(f32[98304]{0:T(1024)S(1)} %reshape.70, s32[8192]{0:T(1024)S(1)} %broadcast_clamp_fusion.2), kind=kCustom, calls=%fused_computation | custom fusion | bytes 98304 | tf_op jit(solution)/shard_map/gather | solution.py:102
  535.4 45.5 %gather_fusion.1 = f32[8192]{0:T(1024)S(1)} fusion(f32[98304]{0:T(1024)S(1)} %reshape.70, s32[8192]{0:T(1024)S(1)} %broadcast_clamp_fusion.1), kind=kCustom, calls=%fused_computation.1 | custom fusion | bytes 98304 | tf_op jit(solution)/shard_map/gather | solution.py:103
  581.0 45.5 %gather_fusion.2 = f32[8192]{0:T(1024)S(1)} fusion(f32[98304]{0:T(1024)S(1)} %reshape.70, s32[8192]{0:T(1024)S(1)} %broadcast_clamp_fusion), kind=kCustom, calls=%fused_computation.2 | custom fusion | bytes 98304 | tf_op jit(solution)/shard_map/gather | solution.py:104
  626.6 0.5 multiply_add_fusion
  627.2 0.1 reduce_sum.37
  627.3 0.7 multiply_reduce_fusion.1
  627.9 124.3 %all-reduce = (f32[]{:T(128)}, f32[]{:T(128)}) all-reduce(f32[]{:T(128)} %get-tuple-element.36, f32[]{:T(128)} %get-tuple-element.9), channel_id=1, replica_groups=mesh['tm'=4,'det'=64] {'det'}, use_global_device_ids=true, to_apply=%region_1.2 | all-reduce | flops 2 | bytes 16 | tf_op jit(solution)/shard_map/psum | solution.py:12
  752.2 9.1 %all-reduce.1 = (f32[]{:T(128)}, f32[]{:T(128)}) all-reduce(f32[]{:T(128)} %get-tuple-element.3, f32[]{:T(128)} %get-tuple-element.4), channel_id=1, replica_groups=mesh['tm'=4,'det'=64] {'tm'}, use_global_device_ids=true, to_apply=%region_2.3 | all-reduce | flops 2 | bytes 16 | tf_op jit(solution)/shard_map/psum | solution.py:13
  762.6 0.6 multiply_reduce_fusion
  763.2 75.3 %psum.47 = f32[]{:T(128)} all-reduce(f32[]{:T(128)} %get-tuple-element.7), channel_id=1, replica_groups=mesh['tm'=4,'det'=64] {'tm','det'}, use_global_device_ids=true, to_apply=%region_11.12 | all-reduce | flops 1 | bytes 8 | tf_op jit(solution)/shard_map/psum | solution.py:122
  839.9 0.6 multiply_add_fusion.1
  (44 shorter events, 0.7 us)
Async XLA Ops:
  7.2 335.8 %reduce-scatter.2.cloned.1.call-start = ((), (), s32[]{:S(2)}) async-start(), calls=%async_computation.1 | async-start | bytes 9584640 | tf_op jit(solution)/shard_map/reduce_scatter | solution.py:91
  181.6 163.1 %copy-start = (f32[48,6,256]{2,0,1:T(8,128)S(1)}, f32[48,6,256]{2,0,1:T(8,128)}, u32[]{:S(2)}) copy-start(f32[48,6,256]{2,0,1:T(8,128)} %param.15) | copy-start | bytes 884740
  187.8 207.1 %copy-start.2 = (f32[2,4]{1,0:T(2,128)S(1)}, f32[2,4]{1,0:T(2,128)}, u32[]{:S(2)}) copy-start(f32[2,4]{1,0:T(2,128)} %param.10) | copy-start | bytes 100
  187.8 204.8 %all-reduce.4.cloned.1.call-start = ((), (), s32[]{:S(2)}) async-start(), calls=%async_computation.2 | async-start | bytes 393216 | tf_op jit(solution)/shard_map/psum | solution.py:92
  344.6 137.9 %all-gather.2.cloned.1.call-start = ((), (), s32[]{:S(2)}) async-start(), calls=%async_computation.3 | async-start | bytes 9584640 | tf_op jit(solution)/shard_map/all_gather | solution.py:96
  395.0 3.6 collective-permute-start
  397.2 4.4 collective-permute-start.1
  581.0 45.6 %copy-start.1 = (f32[2,4096]{1,0:T(2,128)S(1)}, f32[2,4096]{1,0:T(2,128)}, u32[]{:S(2)}) copy-start(f32[2,4096]{1,0:T(2,128)} %param.12) | copy-start | bytes 98308
  581.0 46.2 %copy-start.3 = (f32[2,4]{1,0:T(2,128)S(1)}, f32[2,4]{1,0:T(2,128)}, u32[]{:S(2)}) copy-start(f32[2,4]{1,0:T(2,128)} %param.9) | copy-start | bytes 100
  581.0 258.8 %copy-start.5 = (f32[2,4]{1,0:T(2,128)S(1)}, f32[2,4]{1,0:T(2,128)}, u32[]{:S(2)}) copy-start(f32[2,4]{1,0:T(2,128)} %param.8) | copy-start | bytes 100
  763.2 77.2 %copy-start.4 = (f32[2,4]{1,0:T(2,128)}, f32[2,4]{1,0:T(2,128)S(1)}, u32[]{:S(2)}) copy-start(f32[2,4]{1,0:T(2,128)S(1)} %get-tuple-element.8) | copy-start | bytes 100
Sparse Core Ops, SparseCore 0:
  187.9 154.9 reduce-scatter.1
  345.3 47.3 all-reduce.3
  395.4 87.0 all-gather.1
